TPU v7x, 32 devices: a whole 2x2x4 slice. The times are simulated.
32 devices in a mesh: wide: 16 (over z, x, core), narrow: 2 (over y).
Axes of the slice: x: 2, y: 2, z: 4, core: 2. Of those that a mesh axis runs over, the one named last changes fastest.
Arguments:
- amplitudes: float32 [48, 1024, 1024], P('wide', None, 'narrow'), may hold values from -24 to 24
- integrals: float32 [16, 16, 1024, 1024], P('narrow', None, 'wide'), may hold values from -0.005859375 to 0.005859375
- pair_index: int32 [48, 2], P('wide'), may hold values from 0 to 199
- window_virtuals: int32 [16], replicated, may hold values from 0 to 1023
- occ_energy: float32 [200], replicated, may hold values from -3 to -0.5
- virt_energy: float32 [1024], replicated, may hold values from 0.3 to 6
Outputs:
- update: float32 [16, 16, 48], P('narrow', None, 'wide')
All inputs are finite; a program needn't handle non-finite values.
Results may differ from a plain program's by a relative error of at most 0.00013.
Values sent between devices are 32-bit elements; how exact they have to be, the bound alone decides.
No kernel may reach another device: no remote copies, remote signals or barrier semaphores. Data moves between devices by JAX's collectives and lax.ppermute only.
A program may use at most 128 MiB of HBM per device.

v0:
```python
import jax
import jax.numpy as jnp
from jax import lax
from jax.sharding import PartitionSpec as P


def lookup(table, indices):
    matches = (indices[..., None] == jnp.arange(table.shape[0], dtype=jnp.int32)).astype(
        jnp.float32
    )
    return jnp.sum(matches * table, axis=-1)


def contract(left_rows, right_rows):
    return lax.dot_general(
        left_rows.reshape(left_rows.shape[0], -1),
        right_rows.reshape(right_rows.shape[0], -1),
        (((1,), (1,)), ((), ())),
        precision=lax.Precision.HIGHEST,
        preferred_element_type=jnp.float32,
    )


def shards(amplitudes, integrals, pair_index, window_virtuals, occ_energy, virt_energy):
    exchanged = lax.all_to_all(amplitudes, "wide", split_axis=1, concat_axis=0, tiled=True)
    rows_here = integrals.shape[0]
    window = integrals.shape[1]
    first_block = integrals.shape[2]
    all_pairs = exchanged.shape[0]
    integral_rows = integrals.reshape(rows_here * window, first_block, integrals.shape[3])
    partial_value = contract(integral_rows, lax.all_gather(exchanged, "narrow", axis=2, tiled=True))
    ladder = lax.psum_scatter(
        partial_value.reshape(rows_here, window, all_pairs), "wide", scatter_dimension=2, tiled=True
    )
    swapped = lax.all_to_all(ladder, "narrow", split_axis=1, concat_axis=0, tiled=True)
    combined = ladder + jnp.transpose(swapped, (1, 0, 2))
    row_start = lax.axis_index("narrow") * rows_here
    own_virtuals = lax.dynamic_slice_in_dim(window_virtuals, row_start, rows_here, 0)
    row_energy = lookup(virt_energy, own_virtuals)
    column_energy = lookup(virt_energy, window_virtuals)
    pair_energy = lookup(occ_energy, pair_index[:, 0]) + lookup(occ_energy, pair_index[:, 1])
    denominator = (
        pair_energy[None, None, :] - row_energy[:, None, None] - column_energy[None, :, None]
    )
    return combined / denominator


def solution(mesh):
    in_specs = (
        P("wide", None, "narrow"),
        P("narrow", None, "wide", None),
        P("wide", None),
        P(),
        P(),
        P(),
    )
    out_specs = P("narrow", None, "wide")
    return jax.shard_map(shards, mesh=mesh, in_specs=in_specs, out_specs=out_specs, check_vma=False)
```

profile of v0, /device:TPU:0, one launch (start us, length us, event | category | flops | bytes accessed | tf_op | source)
XLA Modules:
  0.0 489.2 jit_solution(3291001078130395045)
XLA Ops:
  6.5 0.0 all-gather.2.cloned.1.call-start
  6.5 7.1 %copy.42 = f32[3,1024,512]{2,0,1:T(4,128)S(1)} copy(f32[3,1024,512]{2,1,0:T(8,128)} %param.6) | data formatting | bytes 12582912 | tf_op args[0]
  13.6 189.3 %all_to_all.36 = f32[3,1024,512]{2,0,1:T(4,128)S(1)} all-to-all(f32[3,1024,512]{2,0,1:T(4,128)S(1)} %copy.42), channel_id=1, replica_groups=mesh['wide'=16,'narrow'=2] {'wide'}, dimensions={1} | all-to-all | bytes 12582912 | tf_op jit(solution)/shard_map/all_to_all | solution.py:25
  202.9 2.0 copy.43
  205.0 1.2 copy.44
  206.2 0.0 copy-start.3
  206.2 0.0 copy-start.2
  206.2 0.0 copy-start.1
  206.2 0.0 copy-start
  206.3 6.3 %copy.45 = f32[48,64,512]{2,0,1:T(8,128)} copy(f32[48,64,512]{2,1,0:T(8,128)S(1)} %bitcast.30) | data formatting | bytes 12582912 | tf_op jit(solution)/shard_map/all_to_all | solution.py:25
  212.5 0.0 all-gather.2.cloned.1.call-update
  212.5 0.0 reduce-scatter.4.cloned.1.call-start
  212.6 0.0 copy-done.3
  212.6 0.1 dynamic_slice.3
  212.7 0.0 copy-done.2
  212.7 0.0 copy-done.1
  212.7 0.2 select_reduce_fusion.2
  212.9 0.0 copy-done
  212.9 0.2 select_reduce_fusion.1
  213.1 153.1 %all-gather.2.cloned.1.call-done = f32[48,64,1024]{2,0,1:T(8,128)} async-done(((f32[48,64,512]{2,0,1:T(8,128)}), f32[48,64,1024]{2,0,1:T(8,128)}) %all-gather.2.cloned.1.call-update) | async-done | bytes 12582928 | tf_op jit(solution)/shard_map/all_gather | solution.py:31
  366.2 50.3 %fusion.3 = f32[8,16,48]{2,1,0:T(8,128)S(1)} fusion(f32[48,64,1024]{2,0,1:T(8,128)} %all-gather.2.cloned.1.call-done, f32[8,16,64,1024]{3,2,1,0:T(8,128)} %param.7), kind=kOutput, calls=%fused_computation.3 | convolution fusion | flops 4831838208 | bytes 46161920 | tf_op jit(solution)/shard_map/dot_general | solution.py:15
  416.6 0.8 copy.47
  417.4 0.0 reduce-scatter.4.cloned.1.call-update
  417.4 0.1 broadcast_subtract_fusion
  417.5 53.7 %reduce-scatter.4.cloned.1.call-done = f32[8,16,3]{1,0,2:T(8,128)} async-done(((f32[8,16,48]{1,0,2:T(8,128)}), f32[8,16,3]{1,0,2:T(8,128)}) %reduce-scatter.4.cloned.1.call-update) | async-done | bytes 1552
  471.2 0.8 copy.48
  471.9 0.7 reshape.46
  472.6 3.2 all-to-all-start.1
  475.8 0.2 select_reduce_fusion
  476.0 3.6 all-to-all-done.1
  479.6 0.5 broadcast.40
  480.1 0.7 reduce
  480.8 0.1 reshape.47
  480.9 0.1 all_to_all.33
  481.0 1.4 fusion.8
  (3 shorter events, 0.0 us)
Async XLA Ops:
  6.5 359.7 %all-gather.2.cloned.1.call-start = ((), (), s32[]{:S(2)}) async-start(), calls=%async_computation.3 | async-start | bytes 18874368 | tf_op jit(solution)/shard_map/all_gather | solution.py:31
  206.2 6.4 %copy-start.3 = (s32[16]{0:T(128)S(1)}, s32[16]{0:T(128)}, u32[]{:S(2)}) copy-start(s32[16]{0:T(128)} %param.9) | copy-start | bytes 196
  206.2 6.5 %copy-start.2 = (s32[3,2]{0,1:T(2,128)S(1)}, s32[3,2]{0,1:T(2,128)}, u32[]{:S(2)}) copy-start(s32[3,2]{0,1:T(2,128)} %param.8) | copy-start | bytes 76
  206.2 6.5 %copy-start.1 = (f32[200]{0:T(256)S(1)}, f32[200]{0:T(256)}, u32[]{:S(2)}) copy-start(f32[200]{0:T(256)} %param.10) | copy-start | bytes 2404
  206.2 6.7 %copy-start = (f32[1024]{0:T(1024)S(1)}, f32[1024]{0:T(1024)}, u32[]{:S(2)}) copy-start(f32[1024]{0:T(1024)} %param.11) | copy-start | bytes 12292
  212.5 258.6 %reduce-scatter.4.cloned.1.call-start = ((), (), s32[]{:S(2)}) async-start(), calls=%async_computation.4 | async-start | bytes 208896
  472.6 7.0 %all-to-all-start.1 = ((f32[2,1,192]{2,1,0:T(1,128)}), f32[2,1,192]{2,1,0:T(1,128)S(1)}, u32[]{:S(2)}, u32[]{:S(2)}) async-start(f32[2,1,192]{2,1,0:T(1,128)} %reshape.46), calls=%async_computation.1 | async-start | bytes 4096 | tf_op jit(solution)/shard_map/all_to_all | solution.py:35
Sparse Core Ops, SparseCore 0:
  212.7 153.5 all-gather.1
  417.5 53.5 reduce-scatter.3
where the time goes:
time: 490 us; the launch traced here: 489 us
  waiting for transfers between devices  210 us (43%)
  blocking collectives  189 us (39%)
  matrix products  50.3 us (10%)
  local copies, waits for them, and re-layouts  19.7 us (4%)
  between operations  13.5 us (3%)
    all_to_all x1, blocking collectives, shards(): lax.all_to_all(amplitudes, 'wide', split_axis=1, concat_axis=0, tiled=True)  189 us
    all_gather x1, waiting for transfers between devices, shards(): lax.all_gather(exchanged, 'narrow', axis=2, tiled=True)  153 us
    unnamed x3, waiting for transfers between devices  53.7 us
    dot_general x1, matrix products, contract(): lax.dot_general(left_rows.reshape(left_rows.shape[0], -1), right_rows.res...  50.3 us
  transfers between devices with their start and end apart: 3, of which 3 were waited for; matrix products, arithmetic and copies ran while one was open for 0% of the time, Pallas kernels for 0%

commit v1 on v0

--- a/solution.py
+++ b/solution.py
@@ -2,6 +2,12 @@
 import jax.numpy as jnp
 from jax import lax
 from jax.sharding import PartitionSpec as P
+
+
+def trade_parts(x, name, split, join):
+    pieces = jnp.split(x, lax.axis_size(name), axis=split)
+    received = lax.all_to_all(jnp.stack(pieces), name, 0, 0)
+    return jnp.concatenate(received, axis=join)
 
 
 def lookup(table, indices):
@@ -22,7 +28,7 @@
 
 
 def shards(amplitudes, integrals, pair_index, window_virtuals, occ_energy, virt_energy):
-    exchanged = lax.all_to_all(amplitudes, "wide", split_axis=1, concat_axis=0, tiled=True)
+    exchanged = trade_parts(amplitudes, "wide", 1, 0)
     rows_here = integrals.shape[0]
     window = integrals.shape[1]
     first_block = integrals.shape[2]

time: 490 us -> 451 us (0.920)
  local copies, waits for them, and re-layouts: 19.7 us -> 69.2 us
  blocking collectives: 189 us -> 144 us
  waiting for transfers between devices: 210 us -> 177 us
  matrix products: 50.3 us -> 39.2 us
    unnamed x11 -> x27, local copies, waits for them, and re-layouts: 7.9 us -> 65.9 us
    all_to_all x1, blocking collectives: 189 us -> 144 us  [trade_parts(): received = lax.all_to_all(jnp.stack(pieces), name, 0, 0)]
    all_gather x1, waiting for transfers between devices: 153 us -> 120 us  [shards(): lax.all_gather(exchanged, 'narrow', axis=2, tiled=True)]
    dot_general x1, matrix products: 50.3 us -> 39.2 us  [contract(): lax.dot_general(left_rows.reshape(left_rows.shape[0], -1), right_rows.res...]
    all_to_all x3 -> x0, local copies, waits for them, and re-layouts: 9.52 us -> none  [shards(): lax.all_to_all(amplitudes, 'wide', split_axis=1, concat_axis=0, tiled=True)]
  transfers between devices with their start and end apart: 3 -> 3, of which waited for: 3 -> 3; matrix products, arithmetic and copies ran while one was open for 0% -> 8% of each run, Pallas kernels for 0% -> 0%
where the time goes in v1:
time: 451 us; the launch traced here: 449 us
  waiting for transfers between devices  177 us (39%)
  blocking collectives  144 us (32%)
  local copies, waits for them, and re-layouts  69.2 us (15%)
  matrix products  39.2 us (9%)
  between operations  13.6 us (3%)
    all_to_all x1, blocking collectives, trade_parts(): received = lax.all_to_all(jnp.stack(pieces), name, 0, 0)  144 us
    all_gather x1, waiting for transfers between devices, shards(): lax.all_gather(exchanged, 'narrow', axis=2, tiled=True)  120 us
    unnamed x27, local copies, waits for them, and re-layouts  65.9 us
    unnamed x3, waiting for transfers between devices  53.7 us
    dot_general x1, matrix products, contract(): lax.dot_general(left_rows.reshape(left_rows.shape[0], -1), right_rows.res...  39.2 us
  transfers between devices with their start and end apart: 3, of which 3 were waited for; matrix products, arithmetic and copies ran while one was open for 8% of the time, Pallas kernels for 0%

profile of v1, /device:TPU:0, one launch (start us, length us, event | category | flops | bytes accessed | tf_op | source)
XLA Modules:
  0.0 449.4 jit_solution(14589296256108769780)
XLA Ops:
  6.5 0.0 all-gather.2.cloned.1.call-start
  6.5 1.0 bitcast_dynamic-update-slice_fusion.15
  7.6 1.0 bitcast_dynamic-update-slice_fusion.14
  8.6 1.0 bitcast_dynamic-update-slice_fusion.13
  9.6 1.0 bitcast_dynamic-update-slice_fusion.12
  10.7 1.0 bitcast_dynamic-update-slice_fusion.11
  11.7 1.0 bitcast_dynamic-update-slice_fusion.10
  12.7 1.0 bitcast_dynamic-update-slice_fusion.9
  13.8 1.0 bitcast_dynamic-update-slice_fusion.8
  14.8 1.0 bitcast_dynamic-update-slice_fusion.7
  15.8 1.0 bitcast_dynamic-update-slice_fusion.6
  16.9 1.0 bitcast_dynamic-update-slice_fusion.5
  17.9 1.0 bitcast_dynamic-update-slice_fusion.4
  18.9 1.0 bitcast_dynamic-update-slice_fusion.3
  20.0 1.0 bitcast_dynamic-update-slice_fusion.2
  21.0 1.0 bitcast_dynamic-update-slice_fusion.1
  22.0 1.0 bitcast_dynamic-update-slice_fusion
  23.1 144.5 %all_to_all.23 = f32[16,3,64,512]{3,2,1,0:T(8,128)} all-to-all(f32[16,3,64,512]{3,2,1,0:T(8,128)S(1)} %bitcast_dynamic-update-slice_fusion), channel_id=1, replica_groups=mesh['wide'=16,'narrow'=2] {'wide'}, dimensions={0} | all-to-all | bytes 12582912 | tf_op jit(solution)/shard_map/all_to_all | solution.py:9
  167.5 0.0 all-gather.2.cloned.1.call-update
  167.6 0.0 reduce-scatter.4.cloned.1.call-start
  167.6 0.0 copy-start.3
  167.6 0.0 copy-start.2
  167.6 0.0 copy-start.1
  167.6 0.0 copy-start
  167.7 33.2 %copy.20 = f32[16,8,64,1024]{3,1,2,0:T(8,128)} copy(f32[16,8,64,1024]{3,2,1,0:T(8,128)} %bitcast.62) | data formatting | bytes 67108864
  200.8 0.0 copy-done.3
  200.8 0.1 dynamic_slice.3
  200.9 0.0 copy-done.2
  200.9 0.0 copy-done.1
  200.9 0.2 select_reduce_fusion.2
  201.1 0.0 copy-done
  201.2 0.2 select_reduce_fusion.1
  201.3 119.7 %all-gather.2.cloned.1.call-done = f32[48,64,1024]{2,1,0:T(8,128)} async-done(((f32[48,64,512]{2,1,0:T(8,128)}), f32[48,64,1024]{2,1,0:T(8,128)}) %all-gather.2.cloned.1.call-update) | async-done | bytes 12582928 | tf_op jit(solution)/shard_map/all_gather | solution.py:37
  321.1 16.4 %copy.19 = f32[6,8,64,1024]{3,1,2,0:T(8,128)} copy(f32[6,8,64,1024]{3,2,1,0:T(8,128)} %bitcast.64) | data formatting | bytes 25165824
  337.5 39.2 %convolution_bitcast_fusion = f32[128,48]{0,1:T(8,128)S(1)} fusion(f32[48,65536]{1,0:T(8,128)} %bitcast.61, f32[128,65536]{1,0:T(8,128)} %bitcast.60), kind=kOutput, calls=%fused_computation | convolution fusion | flops 4831838208 | bytes 46161920 | tf_op jit(solution)/shard_map/dot_general | solution.py:21
  376.7 0.1 copy.15
  376.8 0.8 copy.16
  377.6 0.0 reduce-scatter.4.cloned.1.call-update
  377.6 0.1 broadcast_subtract_fusion
  377.7 53.7 %reduce-scatter.4.cloned.1.call-done = f32[8,16,3]{1,0,2:T(8,128)} async-done(((f32[8,16,48]{1,0,2:T(8,128)}), f32[8,16,3]{1,0,2:T(8,128)}) %reduce-scatter.4.cloned.1.call-update) | async-done | bytes 1552
  431.3 0.8 copy.17
  432.1 0.7 reshape.52
  432.8 3.2 all-to-all-start.1
  436.0 0.2 select_reduce_fusion
  436.2 3.6 all-to-all-done.1
  439.8 0.5 broadcast.40
  440.3 0.7 reduce
  441.0 0.1 reshape.53
  441.1 0.1 all_to_all.20
  441.2 1.4 fusion
  (3 shorter events, 0.0 us)
Async XLA Ops:
  6.5 314.5 %all-gather.2.cloned.1.call-start = ((), (), s32[]{:S(2)}) async-start(), calls=%async_computation.3 | async-start | bytes 18874368 | tf_op jit(solution)/shard_map/all_gather | solution.py:37
  167.6 263.8 %reduce-scatter.4.cloned.1.call-start = ((), (), s32[]{:S(2)}) async-start(), calls=%async_computation.4 | async-start | bytes 208896
  167.6 33.2 %copy-start.3 = (s32[16]{0:T(128)S(1)}, s32[16]{0:T(128)}, u32[]{:S(2)}) copy-start(s32[16]{0:T(128)} %param.9) | copy-start | bytes 196
  167.6 33.3 %copy-start.2 = (s32[3,2]{0,1:T(2,128)S(1)}, s32[3,2]{0,1:T(2,128)}, u32[]{:S(2)}) copy-start(s32[3,2]{0,1:T(2,128)} %param.8) | copy-start | bytes 76
  167.6 33.3 %copy-start.1 = (f32[200]{0:T(256)S(1)}, f32[200]{0:T(256)}, u32[]{:S(2)}) copy-start(f32[200]{0:T(256)} %param.10) | copy-start | bytes 2404
  167.6 33.5 %copy-start = (f32[1024]{0:T(1024)S(1)}, f32[1024]{0:T(1024)}, u32[]{:S(2)}) copy-start(f32[1024]{0:T(1024)} %param.11) | copy-start | bytes 12292
  432.8 7.0 %all-to-all-start.1 = ((f32[2,1,192]{2,1,0:T(1,128)}), f32[2,1,192]{2,1,0:T(1,128)S(1)}, u32[]{:S(2)}, u32[]{:S(2)}) async-start(f32[2,1,192]{2,1,0:T(1,128)} %reshape.52), calls=%async_computation.1 | async-start | bytes 4096 | tf_op jit(solution)/shard_map/all_to_all | solution.py:41
Sparse Core Ops, SparseCore 0:
  167.7 153.3 all-gather.1
  377.7 53.5 reduce-scatter.3
